TPU v7x, 256 devices: a whole 4x4x8 slice. The times are simulated.
256 devices in a mesh: row: 16 (over z, core), col: 16 (over y, x).
Axes of the slice: x: 4, y: 4, z: 8, core: 2. Of those that a mesh axis runs over, the one named last changes fastest.
Arguments:
- tiles: bfloat16 [16, 16, 16, 512, 512], P('row', 'col'), as said below
- tile_rows: int32 [16, 16, 16], P('row', 'col'), may hold values from 0 to 11, as said below
- tile_cols: int32 [16, 16, 16], P('row', 'col'), may hold values from 0 to 11
- tile_counts: int32 [16, 16], P('row', 'col'), may hold values from 4 to 16, as said below
- sketch: bfloat16 [98304, 256], P(('row', 'col')), as said below
Outputs:
- basis: float32 [98304, 256], P(('row', 'col'))
- factor: float32 [256, 256], replicated
Inputs may be any that keep to these rules, and one draw needn't show every extreme that they name: Within one device's slots the pairs (tile_rows, tile_cols) are all different. `tile_counts`: some device uses all 16 slots in every draw. `tiles`: real valued tile entries of order one over the square root of a row's fan-in. `sketch`: real valued entries of order one.
All inputs are finite; a program needn't handle non-finite values.
Results may differ from a plain program's by a relative error of at most 0.0023.
Values may be sent and summed in bfloat16 or wider, within the bound.
A program may use at most 64 MiB of HBM per device.

v0:
```python
import jax
import jax.numpy as jnp
from jax import lax
from jax.sharding import PartitionSpec as P

BR = 12
BC = 12


def body(tiles, tile_rows, tile_cols, tile_counts, sketch):
    tile_size = tiles.shape[-1]
    sketch_width = sketch.shape[1]
    local_tiles = tiles[0, 0]
    row_ids = tile_rows[0, 0]
    col_ids = tile_cols[0, 0]
    live_count = tile_counts[0, 0]
    gathered = lax.all_gather(sketch, "col", axis=0, tiled=True)

    def transposed_step(slot_index, running):
        matrix = lax.dynamic_index_in_dim(local_tiles, slot_index, 0, keepdims=False)
        sketch_block = lax.dynamic_slice_in_dim(
            gathered, row_ids[slot_index] * tile_size, tile_size, 0
        )
        product = lax.dot_general(
            matrix, sketch_block, (((0,), (0,)), ((), ())), preferred_element_type=jnp.float32
        )
        target = col_ids[slot_index] * tile_size
        current = lax.dynamic_slice_in_dim(running, target, tile_size, 0)
        return lax.dynamic_update_slice_in_dim(running, current + product, target, 0)

    partial_cols = lax.fori_loop(
        0, live_count, transposed_step, jnp.zeros((BC * tile_size, sketch_width), jnp.float32)
    )
    shared = lax.psum_scatter(partial_cols, "row", scatter_dimension=0, tiled=True).astype(
        jnp.bfloat16
    )
    columns = lax.all_gather(shared, "row", axis=0, tiled=True)

    def forward_step(slot_index, running):
        matrix = lax.dynamic_index_in_dim(local_tiles, slot_index, 0, keepdims=False)
        column_block = lax.dynamic_slice_in_dim(
            columns, col_ids[slot_index] * tile_size, tile_size, 0
        )
        product = jnp.dot(matrix, column_block, preferred_element_type=jnp.float32)
        target = row_ids[slot_index] * tile_size
        current = lax.dynamic_slice_in_dim(running, target, tile_size, 0)
        return lax.dynamic_update_slice_in_dim(running, current + product, target, 0)

    partial_rows = lax.fori_loop(
        0, live_count, forward_step, jnp.zeros((BR * tile_size, sketch_width), jnp.float32)
    )
    owned_rows = lax.psum_scatter(partial_rows, "col", scatter_dimension=0, tiled=True)
    total_rows = BR * tile_size * lax.axis_size("row")
    local_gram = jnp.dot(
        owned_rows.T,
        owned_rows,
        precision=lax.Precision.HIGHEST,
        preferred_element_type=jnp.float32,
    )
    gram_matrix = lax.psum(local_gram, ("row", "col")) / total_rows
    cholesky_lower = jnp.linalg.cholesky(gram_matrix)
    basis_rows = lax.linalg.triangular_solve(
        cholesky_lower, owned_rows, left_side=False, lower=True, transpose_a=True
    )
    return (basis_rows, cholesky_lower.T)


def solution(mesh):
    return jax.shard_map(
        body,
        mesh=mesh,
        in_specs=(
            P("row", "col", None, None, None),
            P("row", "col", None),
            P("row", "col", None),
            P("row", "col"),
            P(("row", "col"), None),
        ),
        out_specs=(P(("row", "col"), None), P()),
        check_vma=False,
    )
```

profile of v0, /device:TPU:2, one launch (start us, length us, event | category | flops | bytes accessed | tf_op | source)
XLA Modules:
  0.0 780.2 jit_solution(2374643312332918244)
XLA Ops:
  8.0 57.3 %all-gather.3.cloned.1.call-done = bf16[6144,256]{1,0:T(8,128)(2,1)} async-done(((bf16[384,256]{1,0:T(8,128)(2,1)}), bf16[6144,256]{1,0:T(8,128)(2,1)}) %all-gather.3.cloned.1.call-update) | async-done | bytes 3145744 | tf_op jit(solution)/shard_map/all_gather | solution.py:17
  65.2 3.1 broadcast.98.clone
  68.3 47.2 %while.21 = (s32[]{:T(128)}, f32[6144,256]{1,0:T(8,128)}, s32[]{:T(128)}, s32[16]{0:T(128)S(1)}, bf16[16,512,512]{2,1,0:T(8,128)(2,1)}, /*index=5*/s32[16]{0:T(1...) while((s32[]{:T(128)}, f32[6144,256]{1,0:T(8,128)}, ...), condition=%wide.region_1.2_spmd, body=%wide.region_0.1_spmd.sunk | while | flops 134348816 | bytes 1835287 | solution.py:31
  71.7 2.4 fusion.37
  77.5 2.4 fusion.37
  83.3 2.4 fusion.37
  89.1 2.4 fusion.37
  95.0 2.4 fusion.37
  100.8 2.4 fusion.37
  106.6 2.4 fusion.37
  112.4 2.4 fusion.37
  115.6 113.3 %reduce-scatter.3.cloned.1.call-done = f32[384,256]{1,0:T(8,128)} async-done(((f32[6144,256]{1,0:T(8,128)}), f32[384,256]{1,0:T(8,128)}) %reduce-scatter.3.cloned.1.call-update) | async-done | bytes 393232 | tf_op jit(solution)/shard_map/reduce_scatter | solution.py:34
  230.6 39.8 %all-gather.5.cloned.1.call-done = bf16[6144,256]{1,0:T(8,128)(2,1)} async-done(((bf16[384,256]{1,0:T(8,128)(2,1)}), bf16[6144,256]{1,0:T(8,128)(2,1)}) %all-gather.5.cloned.1.call-update) | async-done | bytes 3145744 | tf_op jit(solution)/shard_map/all_gather | solution.py:37
  270.4 3.1 broadcast.98
  273.5 45.0 %while.22 = (s32[]{:T(128)}, f32[6144,256]{1,0:T(8,128)}, s32[]{:T(128)}, s32[16]{0:T(128)S(1)}, bf16[16,512,512]{2,1,0:T(8,128)(2,1)}, /*index=5*/s32[16]{0:T(1...) while((s32[]{:T(128)}, f32[6144,256]{1,0:T(8,128)}, ...), condition=%wide.region_4.5_spmd, body=%wide.region_3.4_spmd.sunk | while | flops 134348816 | bytes 1835287 | solution.py:49
  287.7 2.4 fusion.40
  318.6 129.1 %reduce-scatter.5.cloned.1.call-done = f32[384,256]{1,0:T(8,128)} async-done(((f32[6144,256]{1,0:T(8,128)}), f32[384,256]{1,0:T(8,128)}) %reduce-scatter.5.cloned.1.call-update) | async-done | bytes 393232 | tf_op jit(solution)/shard_map/reduce_scatter | solution.py:52
  447.6 2.7 fusion.21
  450.4 257.2 %all-reduce.3.cloned.1.call-done = f32[256,256]{0,1:T(8,128)} async-done(((f32[256,256]{0,1:T(8,128)}), f32[256,256]{0,1:T(8,128)}) %all-reduce.3.cloned.1.call-update) | async-done | bytes 262160 | tf_op jit(solution)/shard_map/psum | solution.py:60
  709.7 11.7 %cholesky.50 = f32[128,128]{1,0:T(8,128)S(1)} custom-call(f32[128,128]{1,0:T(8,128)S(1)} %cholesky.118), custom_call_target="Cholesky" | custom-call | tf_op jit(solution)/shard_map/jit(cholesky)/cholesky | solution.py:61
  721.5 9.8 %custom-call.14 = f32[1,128,128]{1,2,0:T(8,128)S(1)} custom-call(f32[1,128,128]{2,1,0:T(8,128)S(1)} %get-tuple-element.133), custom_call_target="InvertDiagBlocksLowerTriangular" | custom-call | tf_op jit(solution)/shard_map/jit(cholesky)/cholesky | solution.py:61
  731.8 11.7 %cholesky.105 = f32[128,128]{1,0:T(8,128)S(1)} custom-call(f32[128,128]{1,0:T(8,128)S(1)} %convolution_subtract_fusion.1), custom_call_target="Cholesky" | custom-call | tf_op jit(solution)/shard_map/jit(cholesky)/cholesky | solution.py:61
  745.7 4.2 while.23
  750.0 19.7 %custom-call.15 = f32[2,128,128]{1,2,0:T(8,128)S(1)} custom-call(f32[2,128,128]{2,1,0:T(8,128)S(1)} %get-tuple-element.87), custom_call_target="InvertDiagBlocksLowerTriangular" | custom-call | tf_op jit(solution)/shard_map/triangular_solve | solution.py:62
  (82 shorter events, 50.9 us)
Async XLA Ops:
  7.2 61.1 %copy-start.2 = (s32[1,1,16]{2,1,0:T(1,128)S(1)}, s32[1,1,16]{2,1,0:T(1,128)}, u32[]{:S(2)}) copy-start(s32[1,1,16]{2,1,0:T(1,128)} %param.10) | copy-start | bytes 196
  7.2 61.1 %copy-start.1 = (s32[1,1,16]{2,1,0:T(1,128)S(1)}, s32[1,1,16]{2,1,0:T(1,128)}, u32[]{:S(2)}) copy-start(s32[1,1,16]{2,1,0:T(1,128)} %param.11) | copy-start | bytes 196
  7.2 58.0 %all-gather.3.cloned.1.call-start = ((), (), s32[]{:S(2)}) async-start(), calls=%async_computation.2 | async-start | bytes 3342336 | tf_op jit(solution)/shard_map/all_gather | solution.py:17
  7.9 220.9 %reduce-scatter.3.cloned.1.call-start = ((), (), s32[]{:S(2)}) async-start(), calls=%async_computation.3 | async-start | bytes 6684672 | tf_op jit(solution)/shard_map/reduce_scatter | solution.py:34
  115.5 154.9 %all-gather.5.cloned.1.call-start = ((), (), s32[]{:S(2)}) async-start(), calls=%async_computation.4 | async-start | bytes 3342336 | tf_op jit(solution)/shard_map/all_gather | solution.py:37
  230.6 217.1 %reduce-scatter.5.cloned.1.call-start = ((), (), s32[]{:S(2)}) async-start(), calls=%async_computation.5 | async-start | bytes 6684672 | tf_op jit(solution)/shard_map/reduce_scatter | solution.py:52
  318.5 389.1 %all-reduce.3.cloned.1.call-start = ((), (), s32[]{:S(2)}) async-start(), calls=%async_computation.6 | async-start | bytes 524288 | tf_op jit(solution)/shard_map/psum | solution.py:60
  447.6 323.4 %copy-start = (f32[384,256]{1,0:T(8,128)S(1)}, f32[384,256]{1,0:T(8,128)}, u32[]{:S(2)}) copy-start(f32[384,256]{1,0:T(8,128)} %reduce-scatter.5.cloned.1.call-done) | copy-start | bytes 1179652
Sparse Core Ops, SparseCore 0:
  10.4 54.7 all-gather.2
  115.7 113.1 reduce-scatter.2
  231.3 39.0 all-gather.4
  318.6 128.9 reduce-scatter.4
  453.5 254.0 all-reduce.2
where the time goes:
time: 782 us; the launch traced here: 780 us
  waiting for transfers between devices  597 us (76%)
  other arithmetic  57.4 us (7%)
  matrix products  44 us (6%)
  loops' own time  33.8 us (4%)
  local copies, waits for them, and re-layouts  32.2 us (4%)
  between operations  15.3 us (2%)
    psum x1, waiting for transfers between devices, body(): gram_matrix = lax.psum(local_gram, ('row', 'col')) / total_rows  257 us
    reduce_scatter x1, waiting for transfers between devices, body(): lax.psum_scatter(partial_rows, 'col', scatter_dimension=0, tiled=True)  129 us
    reduce_scatter x1, waiting for transfers between devices, body(): lax.psum_scatter(partial_cols, 'row', scatter_dimension=0, tiled=True)  113 us
    all_gather x1, waiting for transfers between devices, body(): gathered = lax.all_gather(sketch, 'col', axis=0, tiled=True)  57.3 us
    all_gather x1, waiting for transfers between devices, body(): columns = lax.all_gather(shared, 'row', axis=0, tiled=True)  39.8 us
    another operation x6, other arithmetic, body(): cholesky_lower = jnp.linalg.cholesky(gram_matrix)  34 us
    another operation x3, other arithmetic, body(): lax.linalg.triangular_solve(cholesky_lower, owned_rows, left_side=False,...  19.7 us
    dot_general x8, matrix products, transposed_step(): lax.dot_general(matrix, sketch_block, (((0,), (0,)), ((), ())), preferred...  19.4 us
  transfers between devices with their start and end apart: 5, of which 5 were waited for; matrix products, arithmetic and copies ran while one was open for 0% of the time, Pallas kernels for 0%

commit v1 on v0

--- a/solution.py
+++ b/solution.py
@@ -5,6 +5,11 @@
 
 BR = 12
 BC = 12
+
+
+def one_after_other(array, axis_one, axis_two):
+    half = lax.psum(array, axis_one)
+    return lax.psum(half, axis_two)
 
 
 def body(tiles, tile_rows, tile_cols, tile_counts, sketch):
@@ -57,7 +62,7 @@
         precision=lax.Precision.HIGHEST,
         preferred_element_type=jnp.float32,
     )
-    gram_matrix = lax.psum(local_gram, ("row", "col")) / total_rows
+    gram_matrix = one_after_other(local_gram, "col", "row") / total_rows
     cholesky_lower = jnp.linalg.cholesky(gram_matrix)
     basis_rows = lax.linalg.triangular_solve(
         cholesky_lower, owned_rows, left_side=False, lower=True, transpose_a=True

time: 782 us -> 733 us (0.937)
  waiting for transfers between devices: 597 us -> 547 us
    psum x1 -> x2, waiting for transfers between devices: 257 us -> 207 us  [the longest x1 112 us: one_after_other(): return lax.psum(half, axis_two)]
  transfers between devices with their start and end apart: 5 -> 6, of which waited for: 5 -> 6; matrix products, arithmetic and copies ran while one was open for 0% -> 0% of each run, Pallas kernels for 0% -> 0%
where the time goes in v1:
time: 733 us; the launch traced here: 730 us
  waiting for transfers between devices  547 us (75%)
  other arithmetic  57.4 us (8%)
  matrix products  43 us (6%)
  loops' own time  33.9 us (5%)
  local copies, waits for them, and re-layouts  32.2 us (4%)
  between operations  15.6 us (2%)
    reduce_scatter x1, waiting for transfers between devices, body(): lax.psum_scatter(partial_rows, 'col', scatter_dimension=0, tiled=True)  129 us
    reduce_scatter x1, waiting for transfers between devices, body(): lax.psum_scatter(partial_cols, 'row', scatter_dimension=0, tiled=True)  113 us
    psum x1, waiting for transfers between devices, one_after_other(): return lax.psum(half, axis_two)  112 us
    psum x1, waiting for transfers between devices, one_after_other(): half = lax.psum(array, axis_one)  95.1 us
    all_gather x1, waiting for transfers between devices, body(): gathered = lax.all_gather(sketch, 'col', axis=0, tiled=True)  57.3 us
    all_gather x1, waiting for transfers between devices, body(): columns = lax.all_gather(shared, 'row', axis=0, tiled=True)  39.8 us
    another operation x6, other arithmetic, body(): cholesky_lower = jnp.linalg.cholesky(gram_matrix)  34 us
    another operation x3, other arithmetic, body(): lax.linalg.triangular_solve(cholesky_lower, owned_rows, left_side=False,...  19.7 us
  transfers between devices with their start and end apart: 6, of which 6 were waited for; matrix products, arithmetic and copies ran while one was open for 0% of the time, Pallas kernels for 0%

profile of v1, /device:TPU:2, one launch (start us, length us, event | category | flops | bytes accessed | tf_op | source)
XLA Modules:
  0.0 729.7 jit_solution(5545388819137194925)
XLA Ops:
  8.0 57.3 %all-gather.3.cloned.1.call-done = bf16[6144,256]{1,0:T(8,128)(2,1)} async-done(((bf16[384,256]{1,0:T(8,128)(2,1)}), bf16[6144,256]{1,0:T(8,128)(2,1)}) %all-gather.3.cloned.1.call-update) | async-done | bytes 3145744 | tf_op jit(solution)/shard_map/all_gather | solution.py:22
  65.2 3.1 broadcast.98.clone
  68.3 47.2 %while.21 = (s32[]{:T(128)}, f32[6144,256]{1,0:T(8,128)}, s32[]{:T(128)}, s32[16]{0:T(128)S(1)}, bf16[16,512,512]{2,1,0:T(8,128)(2,1)}, /*index=5*/s32[16]{0:T(1...) while((s32[]{:T(128)}, f32[6144,256]{1,0:T(8,128)}, ...), condition=%wide.region_1.2_spmd, body=%wide.region_0.1_spmd.sunk | while | flops 134348816 | bytes 1835287 | solution.py:36
  71.7 2.4 fusion.37
  77.5 2.4 fusion.37
  83.3 2.4 fusion.37
  89.1 2.4 fusion.37
  95.0 2.4 fusion.37
  100.8 2.4 fusion.37
  106.6 2.4 fusion.37
  112.4 2.4 fusion.37
  115.6 113.3 %reduce-scatter.3.cloned.1.call-done = f32[384,256]{1,0:T(8,128)} async-done(((f32[6144,256]{1,0:T(8,128)}), f32[384,256]{1,0:T(8,128)}) %reduce-scatter.3.cloned.1.call-update) | async-done | bytes 393232 | tf_op jit(solution)/shard_map/reduce_scatter | solution.py:39
  230.6 39.8 %all-gather.5.cloned.1.call-done = bf16[6144,256]{1,0:T(8,128)(2,1)} async-done(((bf16[384,256]{1,0:T(8,128)(2,1)}), bf16[6144,256]{1,0:T(8,128)(2,1)}) %all-gather.5.cloned.1.call-update) | async-done | bytes 3145744 | tf_op jit(solution)/shard_map/all_gather | solution.py:42
  270.4 3.1 broadcast.98
  273.5 45.0 %while.22 = (s32[]{:T(128)}, f32[6144,256]{1,0:T(8,128)}, s32[]{:T(128)}, s32[16]{0:T(128)S(1)}, bf16[16,512,512]{2,1,0:T(8,128)(2,1)}, /*index=5*/s32[16]{0:T(1...) while((s32[]{:T(128)}, f32[6144,256]{1,0:T(8,128)}, ...), condition=%wide.region_4.5_spmd, body=%wide.region_3.4_spmd.sunk | while | flops 134348816 | bytes 1835287 | solution.py:54
  318.6 129.1 %reduce-scatter.5.cloned.1.call-done = f32[384,256]{1,0:T(8,128)} async-done(((f32[6144,256]{1,0:T(8,128)}), f32[384,256]{1,0:T(8,128)}) %reduce-scatter.5.cloned.1.call-update) | async-done | bytes 393232 | tf_op jit(solution)/shard_map/reduce_scatter | solution.py:57
  447.6 2.7 fusion.21
  450.6 95.1 %all-reduce.4.cloned.1.call-done = f32[256,256]{0,1:T(8,128)} async-done(((f32[256,256]{0,1:T(8,128)}), f32[256,256]{0,1:T(8,128)}) %all-reduce.4.cloned.1.call-update) | async-done | bytes 262160 | tf_op jit(solution)/shard_map/psum | solution.py:11
  545.7 111.9 %all-reduce.6.cloned.1.call-done = f32[256,256]{0,1:T(8,128)} async-done(((f32[256,256]{0,1:T(8,128)}), f32[256,256]{0,1:T(8,128)}) %all-reduce.6.cloned.1.call-update) | async-done | bytes 262160 | tf_op jit(solution)/shard_map/psum | solution.py:12
  659.8 11.7 %cholesky.50 = f32[128,128]{1,0:T(8,128)S(1)} custom-call(f32[128,128]{1,0:T(8,128)S(1)} %cholesky.118), custom_call_target="Cholesky" | custom-call | tf_op jit(solution)/shard_map/jit(cholesky)/cholesky | solution.py:66
  671.5 9.8 %custom-call.14 = f32[1,128,128]{1,2,0:T(8,128)S(1)} custom-call(f32[1,128,128]{2,1,0:T(8,128)S(1)} %get-tuple-element.133), custom_call_target="InvertDiagBlocksLowerTriangular" | custom-call | tf_op jit(solution)/shard_map/jit(cholesky)/cholesky | solution.py:66
  681.8 11.7 %cholesky.105 = f32[128,128]{1,0:T(8,128)S(1)} custom-call(f32[128,128]{1,0:T(8,128)S(1)} %convolution_subtract_fusion.1), custom_call_target="Cholesky" | custom-call | tf_op jit(solution)/shard_map/jit(cholesky)/cholesky | solution.py:66
  695.8 4.3 while.23
  700.0 19.7 %custom-call.15 = f32[2,128,128]{1,2,0:T(8,128)S(1)} custom-call(f32[2,128,128]{2,1,0:T(8,128)S(1)} %get-tuple-element.87), custom_call_target="InvertDiagBlocksLowerTriangular" | custom-call | tf_op jit(solution)/shard_map/triangular_solve | solution.py:67
  (85 shorter events, 52.7 us)
Async XLA Ops:
  7.2 61.1 %copy-start.2 = (s32[1,1,16]{2,1,0:T(1,128)S(1)}, s32[1,1,16]{2,1,0:T(1,128)}, u32[]{:S(2)}) copy-start(s32[1,1,16]{2,1,0:T(1,128)} %param.10) | copy-start | bytes 196
  7.2 61.1 %copy-start.1 = (s32[1,1,16]{2,1,0:T(1,128)S(1)}, s32[1,1,16]{2,1,0:T(1,128)}, u32[]{:S(2)}) copy-start(s32[1,1,16]{2,1,0:T(1,128)} %param.11) | copy-start | bytes 196
  7.2 58.0 %all-gather.3.cloned.1.call-start = ((), (), s32[]{:S(2)}) async-start(), calls=%async_computation.2 | async-start | bytes 3342336 | tf_op jit(solution)/shard_map/all_gather | solution.py:22
  7.9 220.9 %reduce-scatter.3.cloned.1.call-start = ((), (), s32[]{:S(2)}) async-start(), calls=%async_computation.3 | async-start | bytes 6684672 | tf_op jit(solution)/shard_map/reduce_scatter | solution.py:39
  115.5 154.9 %all-gather.5.cloned.1.call-start = ((), (), s32[]{:S(2)}) async-start(), calls=%async_computation.4 | async-start | bytes 3342336 | tf_op jit(solution)/shard_map/all_gather | solution.py:42
  230.6 217.1 %reduce-scatter.5.cloned.1.call-start = ((), (), s32[]{:S(2)}) async-start(), calls=%async_computation.5 | async-start | bytes 6684672 | tf_op jit(solution)/shard_map/reduce_scatter | solution.py:57
  318.5 227.2 %all-reduce.4.cloned.1.call-start = ((), (), s32[]{:S(2)}) async-start(), calls=%async_computation.6 | async-start | bytes 524288 | tf_op jit(solution)/shard_map/psum | solution.py:11
  447.6 272.1 %copy-start = (f32[384,256]{1,0:T(8,128)S(1)}, f32[384,256]{1,0:T(8,128)}, u32[]{:S(2)}) copy-start(f32[384,256]{1,0:T(8,128)} %reduce-scatter.5.cloned.1.call-done) | copy-start | bytes 1179652
  450.4 207.3 %all-reduce.6.cloned.1.call-start = ((), (), s32[]{:S(2)}) async-start(), calls=%async_computation.7 | async-start | bytes 524288 | tf_op jit(solution)/shard_map/psum | solution.py:12
Sparse Core Ops, SparseCore 0:
  10.4 54.7 all-gather.2
  115.7 113.1 reduce-scatter.2
  231.3 39.0 all-gather.4
  318.6 128.9 reduce-scatter.4
  451.2 94.4 all-reduce.3
  547.9 109.7 all-reduce.5
